TPU v7x, 256 devices: a whole 4x4x8 slice. The times are simulated.
256 devices in a mesh: half: 2 (over core), dev: 128 (over y, x, z).
Axes of the slice: x: 4, y: 4, z: 8, core: 2. Of those that a mesh axis runs over, the one named last changes fastest.
Arguments:
- field_mix: float32 [32, 32], P('half'), may hold values from -1 to 1
- alm: bfloat16 [1024, 2, 32, 2048], P('dev', None, 'half'), may hold values from -6 to 6
- legendre: bfloat16 [1024, 2048, 128], P('dev'), may hold values from -0.125 to 0.125
- order_ids: int32 [1024], replicated, may hold values from 0 to 1023, each once
- fetch_list: int32 [128, 128, 2], replicated, may hold values from -1 to 31, as said below
- scan_tiles: int32 [512, 32], P('dev'), may hold values from 0 to 255, as said below
- block_tile: int32 [512, 32], P('dev'), may hold values from 0 to 31
- block_pix: int32 [512, 16384], P('dev'), may hold values from -1 to 127, as said below
- noise_kernel: float32 [512, 512], P('dev'), may hold values from -0.24 to 0.24
- scan_weight: float32 [512], P('dev'), may hold values from 0.1 to 1
Outputs:
- binned: float32 [128, 32, 4096], P('dev', 'half')
Inputs may be any that keep to these rules, and one draw needn't show every extreme that they name: `fetch_list`: entry [d, e, k] is the index, among the 32 tiles of device d, of the tile that device e fetches from d in slot k, or -1 for an empty slot; the live slots of one pair come first and name distinct tiles; every device fills all 2 slots from at least one source. `scan_tiles`: entry [n, i] is a slot source 2 + k whose fetch_list[source, n div 4, k] is not -1. `block_pix`: -1 marks a flagged sample.
All inputs are finite; a program needn't handle non-finite values.
Results may differ from a plain program's by a relative error of at most 0.007.
Values may be sent and summed in bfloat16 or wider, within the bound.
No kernel may reach another device: no remote copies, remote signals or barrier semaphores. Data moves between devices by JAX's collectives and lax.ppermute only.
A program may use at most 128 MiB of HBM per device.

v0:
```python
import math
import jax
import jax.numpy as jnp
from jax import lax
from jax.sharding import PartitionSpec as P

NPHI = 4096
TILE = 128
BLK = 512


def toeplitz_rows(band_values, block_len):
    scan_count = band_values.shape[0]
    wrapped = jnp.pad(band_values, ((0, 0), (0, 1)))
    repeated = jnp.tile(wrapped, (1, block_len))
    folded = repeated[:, : block_len * (2 * block_len - 1)].reshape(
        scan_count, block_len, 2 * block_len - 1
    )
    return folded[:, :, block_len - 1 :]


def local(
    field_mix,
    alm,
    legendre,
    order_ids,
    fetch_list,
    scan_tiles,
    block_tile,
    block_pix,
    noise_kernel,
    scan_weight,
):
    highest = lax.Precision.HIGHEST
    device_count = lax.axis_size("dev")
    position = lax.axis_index("dev")
    both_halves = lax.all_gather(alm, "half", axis=2, tiled=True)
    mixed_alm = jnp.einsum(
        "fg,scgl->scfl", field_mix, both_halves.astype(jnp.float32), precision=highest
    ).astype(jnp.bfloat16)
    cycle_coeff = jnp.einsum(
        "scfl,slr->rscf", mixed_alm, legendre, preferred_element_type=jnp.float32
    ).astype(jnp.bfloat16)
    by_cycle = lax.all_to_all(cycle_coeff, "dev", split_axis=0, concat_axis=1, tiled=True)
    cycle_count = by_cycle.shape[0]
    order_count = by_cycle.shape[1]
    field_count = by_cycle.shape[3]
    pixel_block = 512
    block_count = NPHI // pixel_block
    weights = jnp.where(order_ids == 0, 1.0, 2.0).astype(jnp.float32) / math.sqrt(2.0 * order_count)

    def cycle_block(start):
        pixel_iota = start + jnp.arange(pixel_block, dtype=jnp.int32)
        phase_steps = order_ids[:, None] * (2 * pixel_iota[None, :] + 1) % (2 * NPHI)
        angles = phase_steps.astype(jnp.float32) * (math.pi / NPHI)
        fourier = jnp.stack(
            [weights[:, None] * jnp.cos(angles), -weights[:, None] * jnp.sin(angles)], axis=1
        ).astype(jnp.bfloat16)
        return jnp.einsum(
            "rscf,scj->rfj", by_cycle, fourier, preferred_element_type=jnp.float32
        ).astype(jnp.bfloat16)

    starts = jnp.arange(block_count, dtype=jnp.int32) * pixel_block
    cycle_blocks = lax.map(cycle_block, starts)
    per_block = pixel_block // TILE
    map_tiles = cycle_blocks.reshape(block_count, cycle_count, field_count, per_block, TILE)
    map_tiles = map_tiles.transpose(1, 0, 3, 2, 4).reshape(
        cycle_count * block_count * per_block, field_count, TILE
    )
    tile_count = map_tiles.shape[0]
    slot_capacity = fetch_list.shape[2]
    owner_row = lax.dynamic_index_in_dim(fetch_list, position, 0, keepdims=False)
    every_tile = lax.all_gather(map_tiles, "dev", axis=0, tiled=True)
    my_column = lax.dynamic_index_in_dim(fetch_list, position, 1, keepdims=False)
    global_ids = jnp.arange(device_count, dtype=jnp.int32)[:, None] * tile_count + jnp.maximum(
        my_column, 0
    )
    fetched = every_tile[global_ids] * (my_column >= 0).astype(jnp.bfloat16)[:, :, None, None]
    slot_total = device_count * slot_capacity
    flat_fetched = fetched.reshape(slot_total, field_count, TILE)
    scan_count = block_tile.shape[0]
    block_total = block_tile.shape[1]
    slot_index = jnp.take_along_axis(scan_tiles, block_tile, axis=1)
    block_tiles = flat_fetched[slot_index]
    pixels = block_pix.reshape(scan_count, block_total, BLK)
    one_hot = (
        pixels[:, :, None, :] == jnp.arange(TILE, dtype=jnp.int32)[None, None, :, None]
    ).astype(jnp.bfloat16)
    samples = jnp.einsum(
        "sbfp,sbpt->sbft", block_tiles, one_hot, preferred_element_type=jnp.float32
    ).astype(jnp.bfloat16)
    taps = noise_kernel.astype(jnp.bfloat16)
    near_band = jnp.concatenate([taps[:, ::-1], taps[:, 1:]], axis=1)
    far_band = jnp.concatenate(
        [jnp.zeros((scan_count, BLK), jnp.bfloat16), taps[:, 1:][:, ::-1]], axis=1
    )
    near_table = toeplitz_rows(near_band, BLK)
    far_table = toeplitz_rows(far_band, BLK)
    earlier = jnp.pad(samples[:, :-1], ((0, 0), (1, 0), (0, 0), (0, 0)))
    later = jnp.pad(samples[:, 1:], ((0, 0), (0, 1), (0, 0), (0, 0)))
    filtered = jnp.einsum("sbfu,stu->sbft", samples, near_table, preferred_element_type=jnp.float32)
    filtered = filtered + jnp.einsum(
        "sbfu,stu->sbft", earlier, far_table, preferred_element_type=jnp.float32
    )
    filtered = filtered + jnp.einsum(
        "sbfu,sut->sbft", later, far_table, preferred_element_type=jnp.float32
    )
    weighted = (scan_weight[:, None, None, None] * filtered).astype(jnp.bfloat16)
    partial_value = jnp.einsum(
        "sbft,sbpt->sbfp", weighted, one_hot, preferred_element_type=jnp.float32
    )
    flat_slots = slot_index.reshape(-1)
    slot_select = (jnp.arange(slot_total, dtype=jnp.int32)[:, None] == flat_slots[None, :]).astype(
        jnp.float32
    )
    per_slot = jnp.dot(
        slot_select,
        partial_value.reshape(scan_count * block_total, field_count * TILE),
        precision=highest,
    )
    per_slot = per_slot.reshape(device_count, slot_capacity, field_count, TILE)
    returned = lax.all_to_all(per_slot, "dev", split_axis=0, concat_axis=0, tiled=True)
    owner_select = (
        jnp.arange(tile_count, dtype=jnp.int32)[:, None] == owner_row.reshape(-1)[None, :]
    ).astype(jnp.float32)
    own_tiles = jnp.dot(
        owner_select, returned.reshape(slot_total, field_count * TILE), precision=highest
    )
    binned = own_tiles.reshape(cycle_count, NPHI // TILE, field_count, TILE).transpose(0, 2, 1, 3)
    return binned.reshape(cycle_count, field_count, NPHI)


def solution(mesh):
    return jax.shard_map(
        local,
        mesh=mesh,
        in_specs=(
            P("half", None),
            P("dev", None, "half", None),
            P("dev", None, None),
            P(),
            P(),
            P("dev", None),
            P("dev", None),
            P("dev", None),
            P("dev", None),
            P("dev"),
        ),
        out_specs=P("dev", "half", None),
        check_vma=False,
    )
```

profile of v0, /device:TPU:32, one launch (start us, length us, event | category | flops | bytes accessed | tf_op | source)
XLA Modules:
  0.0 397.4 jit_solution(6174108100497894636)
XLA Ops:
  6.5 0.7 all-gather.3.cloned.1.call-update
  7.3 20.4 %all-gather.3.cloned.1.call-done = bf16[8,2,32,2048]{3,2,1,0:T(8,128)(2,1)} async-done(((bf16[8,2,16,2048]{3,2,1,0:T(8,128)(2,1)}), bf16[8,2,32,2048]{3,2,1,0:T(8,128)(2,1)}) %all-gather.3.cloned.1.call-update) | async-done | bytes 2097168 | tf_op jit(solution)/shard_map/all_gather | solution.py:37
  27.7 2.8 fusion.27
  30.5 3.0 fusion.36
  33.9 1.0 reshape.451
  34.9 13.7 %all-to-all-start = ((bf16[128,2,128]{2,1,0:T(2,128)(2,1)}), bf16[128,2,128]{2,1,0:T(2,128)(2,1)S(1)}, u32[]{:S(2)}, u32[]{:S(2)}) async-start(bf16[128,2,128]{2,1,0:T(2,128)(2,1)} %reshape.451), calls=%async_computation | async-start | bytes 131072 | tf_op jit(solution)/shard_map/all_to_all | solution.py:44
  49.2 10.5 %all-to-all-done = bf16[128,2,128]{2,1,0:T(2,128)(2,1)S(1)} async-done(((bf16[128,2,128]{2,1,0:T(2,128)(2,1)}), bf16[128,2,128]{2,1,0:T(2,128)(2,1)S(1)}, u32[]{:S(2)}, u32[]{:S(2)}) %all-to-all-start) | async-done | bytes 65568 | tf_op jit(solution)/shard_map/all_to_all | solution.py:44
  60.4 88.3 %while.12 = (s32[]{:T(128)}, bf16[8,1,16,512]{3,2,1,0:T(8,128)(2,1)S(1)}, f32[1024]{0:T(1024)S(1)}, s32[1024]{0:T(1024)S(1)}, s32[8]{0:T(128)S(1)}, /*index=5*/f...) while((s32[]{:T(128)}, bf16[8,1,16,512]{3,2,1,0:T(8,128)(2,1)S(1)}, f32[1024]{0:T(1024)S(1)}, ...), condition=%wide.region_1.2_spmd, body=%wide.region_0.1_spmd.sunk | while | flops 44049920 | bytes 4292721 | solution.py:64
  61.0 0.6 multiply_add_fusion.3
  61.6 9.4 %multiply_convert_fusion.4 = (bf16[1024,1,512]{2,0,1:T(8,128)(2,1)S(1)}, bf16[1024,1,512]{2,0,1:T(8,128)(2,1)S(1)}) fusion(s32[512]{0:T(512)S(1)} %multiply_add_fusion.3, s32[1024]{0:T(1024)S(1)} %get-tuple-element.204, f32[1024]{0:T(1024)S(1)} %get-tuple-element.203, f32[1024]{0:T(1024)S(1)} %bitcast.147), kind=kLoop, calls=%fused_computation.16.clone.1 | loop fusion | flops 9437184 | bytes 2111488 | tf_op jit(solution)/shard_map/convert
  72.0 0.6 multiply_add_fusion.3
  72.7 9.4 %multiply_convert_fusion.4 = (bf16[1024,1,512]{2,0,1:T(8,128)(2,1)S(1)}, bf16[1024,1,512]{2,0,1:T(8,128)(2,1)S(1)}) fusion(s32[512]{0:T(512)S(1)} %multiply_add_fusion.3, s32[1024]{0:T(1024)S(1)} %get-tuple-element.204, f32[1024]{0:T(1024)S(1)} %get-tuple-element.203, f32[1024]{0:T(1024)S(1)} %bitcast.147), kind=kLoop, calls=%fused_computation.16.clone.1 | loop fusion | flops 9437184 | bytes 2111488 | tf_op jit(solution)/shard_map/convert
  83.1 0.6 multiply_add_fusion.3
  83.7 9.4 %multiply_convert_fusion.4 = (bf16[1024,1,512]{2,0,1:T(8,128)(2,1)S(1)}, bf16[1024,1,512]{2,0,1:T(8,128)(2,1)S(1)}) fusion(s32[512]{0:T(512)S(1)} %multiply_add_fusion.3, s32[1024]{0:T(1024)S(1)} %get-tuple-element.204, f32[1024]{0:T(1024)S(1)} %get-tuple-element.203, f32[1024]{0:T(1024)S(1)} %bitcast.147), kind=kLoop, calls=%fused_computation.16.clone.1 | loop fusion | flops 9437184 | bytes 2111488 | tf_op jit(solution)/shard_map/convert
  94.1 0.6 multiply_add_fusion.3
  94.8 9.4 %multiply_convert_fusion.4 = (bf16[1024,1,512]{2,0,1:T(8,128)(2,1)S(1)}, bf16[1024,1,512]{2,0,1:T(8,128)(2,1)S(1)}) fusion(s32[512]{0:T(512)S(1)} %multiply_add_fusion.3, s32[1024]{0:T(1024)S(1)} %get-tuple-element.204, f32[1024]{0:T(1024)S(1)} %get-tuple-element.203, f32[1024]{0:T(1024)S(1)} %bitcast.147), kind=kLoop, calls=%fused_computation.16.clone.1 | loop fusion | flops 9437184 | bytes 2111488 | tf_op jit(solution)/shard_map/convert
  105.1 0.6 multiply_add_fusion.3
  105.8 9.4 %multiply_convert_fusion.4 = (bf16[1024,1,512]{2,0,1:T(8,128)(2,1)S(1)}, bf16[1024,1,512]{2,0,1:T(8,128)(2,1)S(1)}) fusion(s32[512]{0:T(512)S(1)} %multiply_add_fusion.3, s32[1024]{0:T(1024)S(1)} %get-tuple-element.204, f32[1024]{0:T(1024)S(1)} %get-tuple-element.203, f32[1024]{0:T(1024)S(1)} %bitcast.147), kind=kLoop, calls=%fused_computation.16.clone.1 | loop fusion | flops 9437184 | bytes 2111488 | tf_op jit(solution)/shard_map/convert
  116.8 9.4 %multiply_convert_fusion.4 = (bf16[1024,1,512]{2,0,1:T(8,128)(2,1)S(1)}, bf16[1024,1,512]{2,0,1:T(8,128)(2,1)S(1)}) fusion(s32[512]{0:T(512)S(1)} %multiply_add_fusion.3, s32[1024]{0:T(1024)S(1)} %get-tuple-element.204, f32[1024]{0:T(1024)S(1)} %get-tuple-element.203, f32[1024]{0:T(1024)S(1)} %bitcast.147), kind=kLoop, calls=%fused_computation.16.clone.1 | loop fusion | flops 9437184 | bytes 2111488 | tf_op jit(solution)/shard_map/convert
  127.9 9.4 %multiply_convert_fusion.4 = (bf16[1024,1,512]{2,0,1:T(8,128)(2,1)S(1)}, bf16[1024,1,512]{2,0,1:T(8,128)(2,1)S(1)}) fusion(s32[512]{0:T(512)S(1)} %multiply_add_fusion.3, s32[1024]{0:T(1024)S(1)} %get-tuple-element.204, f32[1024]{0:T(1024)S(1)} %get-tuple-element.203, f32[1024]{0:T(1024)S(1)} %bitcast.147), kind=kLoop, calls=%fused_computation.16.clone.1 | loop fusion | flops 9437184 | bytes 2111488 | tf_op jit(solution)/shard_map/convert
  138.9 9.4 %multiply_convert_fusion.4 = (bf16[1024,1,512]{2,0,1:T(8,128)(2,1)S(1)}, bf16[1024,1,512]{2,0,1:T(8,128)(2,1)S(1)}) fusion(s32[512]{0:T(512)S(1)} %multiply_add_fusion.3, s32[1024]{0:T(1024)S(1)} %get-tuple-element.204, f32[1024]{0:T(1024)S(1)} %get-tuple-element.203, f32[1024]{0:T(1024)S(1)} %bitcast.147), kind=kLoop, calls=%fused_computation.16.clone.1 | loop fusion | flops 9437184 | bytes 2111488 | tf_op jit(solution)/shard_map/convert
  148.8 0.7 copy.43
  150.9 1.5 gather_fusion.2
  153.3 3.2 copy.59
  156.5 3.1 slice.36
  159.6 5.8 %reshape.447 = bf16[2095104]{0:T(1024)(128)(2,1)} reshape(bf16[4,523776]{1,0:T(4,128)(2,1)} %slice.36) | data formatting | bytes 8380416
  165.4 10.1 %reshape.402 = bf16[4,512,1023]{2,1,0:T(8,128)(2,1)} reshape(bf16[2095104]{0:T(1024)(128)(2,1)} %reshape.447) | data formatting | bytes 8380416 | tf_op jit(solution)/shard_map/reshape | solution.py:16
  176.6 3.2 copy.60
  179.8 3.2 slice.39
  183.0 5.7 %reshape.449 = bf16[2095104]{0:T(1024)(128)(2,1)} reshape(bf16[4,523776]{1,0:T(4,128)(2,1)} %slice.39) | data formatting | bytes 8380416
  188.7 10.1 %reshape.403 = bf16[4,512,1023]{2,1,0:T(8,128)(2,1)} reshape(bf16[2095104]{0:T(1024)(128)(2,1)} %reshape.449) | data formatting | bytes 8380416 | tf_op jit(solution)/shard_map/reshape | solution.py:16
  199.0 93.0 %all-gather.5.cloned.1.call-done = bf16[4096,16,128]{2,1,0:T(8,128)(2,1)} async-done(((bf16[32,16,128]{2,1,0:T(8,128)(2,1)}), bf16[4096,16,128]{2,1,0:T(8,128)(2,1)}) %all-gather.5.cloned.1.call-update) | async-done | bytes 16777232 | tf_op jit(solution)/shard_map/all_gather | solution.py:73
  292.0 6.6 %gather_fusion = bf16[256,16,128]{2,1,0:T(8,128)(2,1)S(1)} fusion(bf16[4096,16,128]{2,1,0:T(8,128)(2,1)} %all-gather.5.cloned.1.call-done, s32[1024]{0:T(1024)S(1)} %pad_clamp_fusion.1), kind=kCustom, calls=%fused_computation | custom fusion | bytes 2098176 | tf_op jit(solution)/shard_map/gather | solution.py:78
  298.9 0.7 gather_fusion.1
  299.6 5.4 %fusion.32 = bf16[4,32,16,512]{3,2,1,0:T(8,128)(2,1)S(1)} fusion(bf16[4,32,16,128]{3,2,1,0:T(8,128)(2,1)S(1)} %bitcast.140, s32[4,32,512]{2,1,0:T(8,128)S(1)} %bitcast.144), kind=kOutput, calls=%fused_computation.43 | convolution fusion | flops 277872640 | bytes 2883584 | tf_op jit(solution)/shard_map/sbfp,sbpt->sbft/dot_general | solution.py:89
  305.0 1.4 fusion.28
  306.4 0.8 copy-done.2
  307.2 1.4 fusion.30
  308.6 1.7 multiply_convert_fusion.2
  310.3 5.0 %fusion.21 = f32[4,32,16,128]{3,2,1,0:T(8,128)S(1)} fusion(bf16[4,32,16,512]{3,2,1,0:T(8,128)(2,1)S(1)} %multiply_convert_fusion.2, s32[4,32,512]{2,1,0:T(8,128)S(1)} %bitcast.145), kind=kOutput, calls=%fused_computation.25 | convolution fusion | flops 276824064 | bytes 3407872 | tf_op jit(solution)/shard_map/sbft,sbpt->sbfp/dot_general | solution.py:109
  316.0 1.0 fusion.39
  317.1 2.5 copy.48
  319.6 11.5 %all-to-all-start.1 = ((f32[128,2,16,128]{3,2,1,0:T(8,128)}), f32[128,2,16,128]{3,2,1,0:T(8,128)S(1)}, u32[]{:S(2)}, u32[]{:S(2)}) async-start(f32[128,2,16,128]{3,2,1,0:T(8,128)} %copy.48), calls=%async_computation.1 | async-start | bytes 4194304 | tf_op jit(solution)/shard_map/all_to_all | solution.py:122
  331.4 52.8 %all-to-all-done.1 = f32[128,2,16,128]{3,2,1,0:T(8,128)S(1)} async-done(((f32[128,2,16,128]{3,2,1,0:T(8,128)}), f32[128,2,16,128]{3,2,1,0:T(8,128)S(1)}, u32[]{:S(2)}, u32[]{:S(2)}) %all-to-all-start.1) | async-done | bytes 2097184 | tf_op jit(solution)/shard_map/all_to_all | solution.py:122
  384.2 2.2 copy.66
  386.4 1.9 copy.49
  388.4 1.1 convolution_bitcast_fusion
  389.5 0.8 reshape.406
  (80 shorter events, 16.2 us)
Async XLA Ops:
  6.5 143.4 %copy-start = (s32[128,128,2]{1,2,0:T(2,128)S(1)}, s32[128,128,2]{1,2,0:T(2,128)}, u32[]{:S(2)}) copy-start(s32[128,128,2]{1,2,0:T(2,128)} %param.16) | copy-start | bytes 393220
  6.5 21.1 %all-gather.3.cloned.1.call-start = ((), (), s32[]{:S(2)}) async-start(), calls=%async_computation.2 | async-start | bytes 3145728 | tf_op jit(solution)/shard_map/all_gather | solution.py:37
  30.4 18.7 %copy-start.5 = (s32[1024]{0:T(1024)S(1)}, s32[1024]{0:T(1024)}, u32[]{:S(2)}) copy-start(s32[1024]{0:T(1024)} %param.15) | copy-start | bytes 12292
  34.9 24.8 %all-to-all-start = ((bf16[128,2,128]{2,1,0:T(2,128)(2,1)}), bf16[128,2,128]{2,1,0:T(2,128)(2,1)S(1)}, u32[]{:S(2)}, u32[]{:S(2)}) async-start(bf16[128,2,128]{2,1,0:T(2,128)(2,1)} %reshape.451), calls=%async_computation | async-start | bytes 131072 | tf_op jit(solution)/shard_map/all_to_all | solution.py:44
  48.6 243.4 %all-gather.5.cloned.1.call-start = ((), (), s32[]{:S(2)}) async-start(), calls=%async_computation.3 | async-start | bytes 16908288 | tf_op jit(solution)/shard_map/all_gather | solution.py:73
  60.4 89.1 %copy-start.6 = (f32[4,512]{1,0:T(4,128)S(1)}, f32[4,512]{1,0:T(4,128)}, u32[]{:S(2)}) copy-start(f32[4,512]{1,0:T(4,128)} %param.20) | copy-start | bytes 24580
  60.4 90.5 %copy-start.7 = (s32[4,32]{1,0:T(4,128)S(1)}, s32[4,32]{1,0:T(4,128)}, u32[]{:S(2)}) copy-start(s32[4,32]{1,0:T(4,128)} %param.18) | copy-start | bytes 1540
  148.7 2.2 copy-start.1
  148.7 3.9 copy-start.4
  299.6 5.4 %copy-start.3 = (bf16[4,512,1023]{2,1,0:T(8,128)(2,1)S(1)}, bf16[4,512,1023]{2,1,0:T(8,128)(2,1)}, u32[]{:S(2)}) copy-start(bf16[4,512,1023]{2,1,0:T(8,128)(2,1)} %reshape.402) | copy-start | bytes 12570628
  305.0 2.2 copy-start.2
  307.2 1.4 copy-start.8
  319.6 64.6 %all-to-all-start.1 = ((f32[128,2,16,128]{3,2,1,0:T(8,128)}), f32[128,2,16,128]{3,2,1,0:T(8,128)S(1)}, u32[]{:S(2)}, u32[]{:S(2)}) async-start(f32[128,2,16,128]{3,2,1,0:T(8,128)} %copy.48), calls=%async_computation.1 | async-start | bytes 4194304 | tf_op jit(solution)/shard_map/all_to_all | solution.py:122
Sparse Core Ops, SparseCore 0:
  9.1 18.5 all-gather.2
  149.6 142.3 all-gather.4
where the time goes:
time: 402 us; the launch traced here: 397 us
  waiting for transfers between devices  177 us (44%)
  other arithmetic  80.8 us (20%)
  local copies, waits for them, and re-layouts  73.3 us (18%)
  matrix products  25.9 us (6%)
  starting transfers between devices  25.8 us (6%)
  between operations  14 us (3%)
    all_gather x1, waiting for transfers between devices, local(): every_tile = lax.all_gather(map_tiles, 'dev', axis=0, tiled=True)  93 us
    another operation x8, other arithmetic  75.2 us
    all_to_all x1, waiting for transfers between devices, local(): lax.all_to_all(per_slot, 'dev', split_axis=0, concat_axis=0, tiled=True)  52.8 us
    unnamed x32, local copies, waits for them, and re-layouts  24.5 us
    all_gather x1, waiting for transfers between devices, local(): both_halves = lax.all_gather(alm, 'half', axis=2, tiled=True)  20.4 us
    reshape x2, local copies, waits for them, and re-layouts, toeplitz_rows(): repeated[:, :block_len * (2 * block_len - 1)]  20.2 us
    all_to_all x1, starting transfers between devices, local(): lax.all_to_all(cycle_coeff, 'dev', split_axis=0, concat_axis=1, tiled=True)  13.7 us
    all_to_all x1, starting transfers between devices, local(): lax.all_to_all(per_slot, 'dev', split_axis=0, concat_axis=0, tiled=True)  11.5 us
  transfers between devices with their start and end apart: 4, of which 4 were waited for; matrix products, arithmetic and copies ran while one was open for 12% of the time, Pallas kernels for 0%

commit v1 on v0

--- a/solution.py
+++ b/solution.py
@@ -34,7 +34,9 @@
     highest = lax.Precision.HIGHEST
     device_count = lax.axis_size("dev")
     position = lax.axis_index("dev")
-    both_halves = lax.all_gather(alm, "half", axis=2, tiled=True)
+    both_halves = jnp.concatenate(
+        lax.all_to_all(jnp.stack([alm] * lax.axis_size("half")), "half", 0, 0), axis=2
+    )
     mixed_alm = jnp.einsum(
         "fg,scgl->scfl", field_mix, both_halves.astype(jnp.float32), precision=highest
     ).astype(jnp.bfloat16)

time: 402 us -> 387 us (0.963)
  waiting for transfers between devices: 177 us -> 156 us
  blocking collectives: 0 us -> 5.42 us
    all_gather x1 -> x0, waiting for transfers between devices: 20.4 us -> none  [local(): both_halves = lax.all_gather(alm, 'half', axis=2, tiled=True)]
    all_to_all x0 -> x1, blocking collectives: none -> 5.42 us  [local(): lax.all_to_all(jnp.stack([alm] * lax.axis_size('half')), 'half', 0, 0)]
    another operation x8 -> x9, other arithmetic: 75.2 us -> 77 us
    unnamed x32 -> x36, local copies, waits for them, and re-layouts: 24.5 us -> 25.2 us
  transfers between devices with their start and end apart: 4 -> 3, of which waited for: 4 -> 3; matrix products, arithmetic and copies ran while one was open for 12% -> 13% of each run, Pallas kernels for 0% -> 0%
where the time goes in v1:
time: 387 us; the launch traced here: 382 us
  waiting for transfers between devices  156 us (40%)
  other arithmetic  82.6 us (21%)
  local copies, waits for them, and re-layouts  74.3 us (19%)
  starting transfers between devices  27.1 us (7%)
  matrix products  22.1 us (6%)
  between operations  14.1 us (4%)
  blocking collectives  5.42 us (1%)
    all_gather x1, waiting for transfers between devices, local(): every_tile = lax.all_gather(map_tiles, 'dev', axis=0, tiled=True)  93 us
    another operation x8, other arithmetic  75.2 us
    all_to_all x1, waiting for transfers between devices, local(): lax.all_to_all(per_slot, 'dev', split_axis=0, concat_axis=0, tiled=True)  52.8 us
    unnamed x36, local copies, waits for them, and re-layouts  25.2 us
    reshape x2, local copies, waits for them, and re-layouts, toeplitz_rows(): repeated[:, :block_len * (2 * block_len - 1)]  20.2 us
    all_to_all x1, starting transfers between devices, local(): lax.all_to_all(cycle_coeff, 'dev', split_axis=0, concat_axis=1, tiled=True)  15 us
    all_to_all x1, starting transfers between devices, local(): lax.all_to_all(per_slot, 'dev', split_axis=0, concat_axis=0, tiled=True)  11.5 us
    all_to_all x1, waiting for transfers between devices, local(): lax.all_to_all(cycle_coeff, 'dev', split_axis=0, concat_axis=1, tiled=True)  10.5 us
  transfers between devices with their start and end apart: 3, of which 3 were waited for; matrix products, arithmetic and copies ran while one was open for 13% of the time, Pallas kernels for 0%

profile of v1, /device:TPU:32, one launch (start us, length us, event | category | flops | bytes accessed | tf_op | source)
XLA Modules:
  0.0 382.0 jit_solution(14745084841799736909)
XLA Ops:
  6.5 1.8 pad_maximum_fusion
  8.3 5.4 %all_to_all.22 = bf16[2,8,2,16,2048]{4,3,2,1,0:T(8,128)(2,1)S(1)} all-to-all(bf16[2,8,2,16,2048]{4,3,2,1,0:T(8,128)(2,1)S(1)} %pad_maximum_fusion), channel_id=1, replica_groups=mesh['half'=2,'dev'=128] {'half'}, dimensions={0} | all-to-all | bytes 4194304 | tf_op jit(solution)/shard_map/all_to_all | solution.py:38
  14.0 1.2 fusion.27
  15.2 0.8 copy-done.4
  15.9 0.8 fusion.36
  17.2 1.0 reshape.459
  18.2 15.0 %all-to-all-start.1 = ((bf16[128,2,128]{2,1,0:T(2,128)(2,1)}), bf16[128,2,128]{2,1,0:T(2,128)(2,1)S(1)}, u32[]{:S(2)}, u32[]{:S(2)}) async-start(bf16[128,2,128]{2,1,0:T(2,128)(2,1)} %reshape.459), calls=%async_computation.1 | async-start | bytes 131072 | tf_op jit(solution)/shard_map/all_to_all | solution.py:46
  33.8 10.5 %all-to-all-done.1 = bf16[128,2,128]{2,1,0:T(2,128)(2,1)S(1)} async-done(((bf16[128,2,128]{2,1,0:T(2,128)(2,1)}), bf16[128,2,128]{2,1,0:T(2,128)(2,1)S(1)}, u32[]{:S(2)}, u32[]{:S(2)}) %all-to-all-start.1) | async-done | bytes 65568 | tf_op jit(solution)/shard_map/all_to_all | solution.py:46
  45.0 88.3 %while.12 = (s32[]{:T(128)}, bf16[8,1,16,512]{3,2,1,0:T(8,128)(2,1)S(1)}, f32[1024]{0:T(1024)S(1)}, s32[1024]{0:T(1024)S(1)}, s32[8]{0:T(128)S(1)}, /*index=5*/f...) while((s32[]{:T(128)}, bf16[8,1,16,512]{3,2,1,0:T(8,128)(2,1)S(1)}, f32[1024]{0:T(1024)S(1)}, ...), condition=%wide.region_1.2_spmd, body=%wide.region_0.1_spmd.sunk | while | flops 44049920 | bytes 4292721 | solution.py:66
  45.6 0.6 multiply_add_fusion.3
  46.2 9.4 %multiply_convert_fusion.4 = (bf16[1024,1,512]{2,0,1:T(8,128)(2,1)S(1)}, bf16[1024,1,512]{2,0,1:T(8,128)(2,1)S(1)}) fusion(s32[512]{0:T(512)S(1)} %multiply_add_fusion.3, s32[1024]{0:T(1024)S(1)} %get-tuple-element.204, f32[1024]{0:T(1024)S(1)} %get-tuple-element.203, f32[1024]{0:T(1024)S(1)} %bitcast.153), kind=kLoop, calls=%fused_computation.16.clone.1 | loop fusion | flops 9437184 | bytes 2111488 | tf_op jit(solution)/shard_map/convert
  56.6 0.6 multiply_add_fusion.3
  57.3 9.4 %multiply_convert_fusion.4 = (bf16[1024,1,512]{2,0,1:T(8,128)(2,1)S(1)}, bf16[1024,1,512]{2,0,1:T(8,128)(2,1)S(1)}) fusion(s32[512]{0:T(512)S(1)} %multiply_add_fusion.3, s32[1024]{0:T(1024)S(1)} %get-tuple-element.204, f32[1024]{0:T(1024)S(1)} %get-tuple-element.203, f32[1024]{0:T(1024)S(1)} %bitcast.153), kind=kLoop, calls=%fused_computation.16.clone.1 | loop fusion | flops 9437184 | bytes 2111488 | tf_op jit(solution)/shard_map/convert
  67.7 0.6 multiply_add_fusion.3
  68.3 9.4 %multiply_convert_fusion.4 = (bf16[1024,1,512]{2,0,1:T(8,128)(2,1)S(1)}, bf16[1024,1,512]{2,0,1:T(8,128)(2,1)S(1)}) fusion(s32[512]{0:T(512)S(1)} %multiply_add_fusion.3, s32[1024]{0:T(1024)S(1)} %get-tuple-element.204, f32[1024]{0:T(1024)S(1)} %get-tuple-element.203, f32[1024]{0:T(1024)S(1)} %bitcast.153), kind=kLoop, calls=%fused_computation.16.clone.1 | loop fusion | flops 9437184 | bytes 2111488 | tf_op jit(solution)/shard_map/convert
  79.4 9.4 %multiply_convert_fusion.4 = (bf16[1024,1,512]{2,0,1:T(8,128)(2,1)S(1)}, bf16[1024,1,512]{2,0,1:T(8,128)(2,1)S(1)}) fusion(s32[512]{0:T(512)S(1)} %multiply_add_fusion.3, s32[1024]{0:T(1024)S(1)} %get-tuple-element.204, f32[1024]{0:T(1024)S(1)} %get-tuple-element.203, f32[1024]{0:T(1024)S(1)} %bitcast.153), kind=kLoop, calls=%fused_computation.16.clone.1 | loop fusion | flops 9437184 | bytes 2111488 | tf_op jit(solution)/shard_map/convert
  90.4 9.4 %multiply_convert_fusion.4 = (bf16[1024,1,512]{2,0,1:T(8,128)(2,1)S(1)}, bf16[1024,1,512]{2,0,1:T(8,128)(2,1)S(1)}) fusion(s32[512]{0:T(512)S(1)} %multiply_add_fusion.3, s32[1024]{0:T(1024)S(1)} %get-tuple-element.204, f32[1024]{0:T(1024)S(1)} %get-tuple-element.203, f32[1024]{0:T(1024)S(1)} %bitcast.153), kind=kLoop, calls=%fused_computation.16.clone.1 | loop fusion | flops 9437184 | bytes 2111488 | tf_op jit(solution)/shard_map/convert
  101.5 9.4 %multiply_convert_fusion.4 = (bf16[1024,1,512]{2,0,1:T(8,128)(2,1)S(1)}, bf16[1024,1,512]{2,0,1:T(8,128)(2,1)S(1)}) fusion(s32[512]{0:T(512)S(1)} %multiply_add_fusion.3, s32[1024]{0:T(1024)S(1)} %get-tuple-element.204, f32[1024]{0:T(1024)S(1)} %get-tuple-element.203, f32[1024]{0:T(1024)S(1)} %bitcast.153), kind=kLoop, calls=%fused_computation.16.clone.1 | loop fusion | flops 9437184 | bytes 2111488 | tf_op jit(solution)/shard_map/convert
  112.5 9.4 %multiply_convert_fusion.4 = (bf16[1024,1,512]{2,0,1:T(8,128)(2,1)S(1)}, bf16[1024,1,512]{2,0,1:T(8,128)(2,1)S(1)}) fusion(s32[512]{0:T(512)S(1)} %multiply_add_fusion.3, s32[1024]{0:T(1024)S(1)} %get-tuple-element.204, f32[1024]{0:T(1024)S(1)} %get-tuple-element.203, f32[1024]{0:T(1024)S(1)} %bitcast.153), kind=kLoop, calls=%fused_computation.16.clone.1 | loop fusion | flops 9437184 | bytes 2111488 | tf_op jit(solution)/shard_map/convert
  122.9 0.6 multiply_add_fusion.3
  123.5 9.4 %multiply_convert_fusion.4 = (bf16[1024,1,512]{2,0,1:T(8,128)(2,1)S(1)}, bf16[1024,1,512]{2,0,1:T(8,128)(2,1)S(1)}) fusion(s32[512]{0:T(512)S(1)} %multiply_add_fusion.3, s32[1024]{0:T(1024)S(1)} %get-tuple-element.204, f32[1024]{0:T(1024)S(1)} %get-tuple-element.203, f32[1024]{0:T(1024)S(1)} %bitcast.153), kind=kLoop, calls=%fused_computation.16.clone.1 | loop fusion | flops 9437184 | bytes 2111488 | tf_op jit(solution)/shard_map/convert
  133.4 0.7 copy.45
  135.5 1.5 gather_fusion.2
  137.9 3.2 copy.61
  141.1 3.1 slice.36
  144.2 5.7 %reshape.455 = bf16[2095104]{0:T(1024)(128)(2,1)} reshape(bf16[4,523776]{1,0:T(4,128)(2,1)} %slice.36) | data formatting | bytes 8380416
  150.0 10.1 %reshape.410 = bf16[4,512,1023]{2,1,0:T(8,128)(2,1)} reshape(bf16[2095104]{0:T(1024)(128)(2,1)} %reshape.455) | data formatting | bytes 8380416 | tf_op jit(solution)/shard_map/reshape | solution.py:16
  161.2 3.2 copy.62
  164.4 3.1 slice.39
  167.6 5.7 %reshape.457 = bf16[2095104]{0:T(1024)(128)(2,1)} reshape(bf16[4,523776]{1,0:T(4,128)(2,1)} %slice.39) | data formatting | bytes 8380416
  173.3 10.1 %reshape.411 = bf16[4,512,1023]{2,1,0:T(8,128)(2,1)} reshape(bf16[2095104]{0:T(1024)(128)(2,1)} %reshape.457) | data formatting | bytes 8380416 | tf_op jit(solution)/shard_map/reshape | solution.py:16
  183.5 93.0 %all-gather.2.cloned.1.call-done = bf16[4096,16,128]{2,1,0:T(8,128)(2,1)} async-done(((bf16[32,16,128]{2,1,0:T(8,128)(2,1)}), bf16[4096,16,128]{2,1,0:T(8,128)(2,1)}) %all-gather.2.cloned.1.call-update) | async-done | bytes 16777232 | tf_op jit(solution)/shard_map/all_gather | solution.py:75
  276.6 6.6 %gather_fusion = bf16[256,16,128]{2,1,0:T(8,128)(2,1)S(1)} fusion(bf16[4096,16,128]{2,1,0:T(8,128)(2,1)} %all-gather.2.cloned.1.call-done, s32[1024]{0:T(1024)S(1)} %pad_clamp_fusion.1), kind=kCustom, calls=%fused_computation | custom fusion | bytes 2098176 | tf_op jit(solution)/shard_map/gather | solution.py:80
  283.5 0.7 gather_fusion.1
  284.2 5.4 %fusion.32 = bf16[4,32,16,512]{3,2,1,0:T(8,128)(2,1)S(1)} fusion(bf16[4,32,16,128]{3,2,1,0:T(8,128)(2,1)S(1)} %bitcast.146, s32[4,32,512]{2,1,0:T(8,128)S(1)} %bitcast.150), kind=kOutput, calls=%fused_computation.44 | convolution fusion | flops 277872640 | bytes 2883584 | tf_op jit(solution)/shard_map/sbfp,sbpt->sbft/dot_general | solution.py:91
  289.6 1.4 fusion.28
  291.0 0.8 copy-done.2
  291.8 1.4 fusion.30
  293.2 1.7 multiply_convert_fusion.2
  294.9 5.0 %fusion.21 = f32[4,32,16,128]{3,2,1,0:T(8,128)S(1)} fusion(bf16[4,32,16,512]{3,2,1,0:T(8,128)(2,1)S(1)} %multiply_convert_fusion.2, s32[4,32,512]{2,1,0:T(8,128)S(1)} %bitcast.151), kind=kOutput, calls=%fused_computation.25 | convolution fusion | flops 276824064 | bytes 3407872 | tf_op jit(solution)/shard_map/sbft,sbpt->sbfp/dot_general | solution.py:111
  300.6 1.0 fusion.39
  301.7 2.5 copy.50
  304.2 11.5 %all-to-all-start.2 = ((f32[128,2,16,128]{3,2,1,0:T(8,128)}), f32[128,2,16,128]{3,2,1,0:T(8,128)S(1)}, u32[]{:S(2)}, u32[]{:S(2)}) async-start(f32[128,2,16,128]{3,2,1,0:T(8,128)} %copy.50), calls=%async_computation.2 | async-start | bytes 4194304 | tf_op jit(solution)/shard_map/all_to_all | solution.py:124
  316.0 52.8 %all-to-all-done.2 = f32[128,2,16,128]{3,2,1,0:T(8,128)S(1)} async-done(((f32[128,2,16,128]{3,2,1,0:T(8,128)}), f32[128,2,16,128]{3,2,1,0:T(8,128)S(1)}, u32[]{:S(2)}, u32[]{:S(2)}) %all-to-all-start.2) | async-done | bytes 2097184 | tf_op jit(solution)/shard_map/all_to_all | solution.py:124
  368.8 2.2 copy.68
  371.1 1.9 copy.51
  373.0 1.1 convolution_bitcast_fusion
  374.1 0.8 reshape.414
  (84 shorter events, 17.1 us)
Async XLA Ops:
  6.5 128.0 %copy-start = (s32[128,128,2]{1,2,0:T(2,128)S(1)}, s32[128,128,2]{1,2,0:T(2,128)}, u32[]{:S(2)}) copy-start(s32[128,128,2]{1,2,0:T(2,128)} %param.16) | copy-start | bytes 393220
  8.3 5.7 %copy-start.7 = (f32[16,32]{1,0:T(8,128)S(1)}, f32[16,32]{1,0:T(8,128)}, u32[]{:S(2)}) copy-start(f32[16,32]{1,0:T(8,128)} %param.12) | copy-start | bytes 6148
  13.7 2.2 copy-start.4
  15.9 17.8 %copy-start.6 = (s32[1024]{0:T(1024)S(1)}, s32[1024]{0:T(1024)}, u32[]{:S(2)}) copy-start(s32[1024]{0:T(1024)} %param.15) | copy-start | bytes 12292
  18.2 26.1 %all-to-all-start.1 = ((bf16[128,2,128]{2,1,0:T(2,128)(2,1)}), bf16[128,2,128]{2,1,0:T(2,128)(2,1)S(1)}, u32[]{:S(2)}, u32[]{:S(2)}) async-start(bf16[128,2,128]{2,1,0:T(2,128)(2,1)} %reshape.459), calls=%async_computation.1 | async-start | bytes 131072 | tf_op jit(solution)/shard_map/all_to_all | solution.py:46
  33.2 243.4 %all-gather.2.cloned.1.call-start = ((), (), s32[]{:S(2)}) async-start(), calls=%async_computation.3 | async-start | bytes 16908288 | tf_op jit(solution)/shard_map/all_gather | solution.py:75
  45.0 89.1 %copy-start.8 = (f32[4,512]{1,0:T(4,128)S(1)}, f32[4,512]{1,0:T(4,128)}, u32[]{:S(2)}) copy-start(f32[4,512]{1,0:T(4,128)} %param.20) | copy-start | bytes 24580
  45.0 90.5 %copy-start.9 = (s32[4,32]{1,0:T(4,128)S(1)}, s32[4,32]{1,0:T(4,128)}, u32[]{:S(2)}) copy-start(s32[4,32]{1,0:T(4,128)} %param.18) | copy-start | bytes 1540
  133.3 2.2 copy-start.1
  133.3 3.9 %copy-start.5 = (s32[4,16384]{1,0:T(4,128)S(1)}, s32[4,16384]{1,0:T(4,128)}, u32[]{:S(2)}) copy-start(s32[4,16384]{1,0:T(4,128)} %param.19) | copy-start | bytes 786436
  284.2 5.4 %copy-start.3 = (bf16[4,512,1023]{2,1,0:T(8,128)(2,1)S(1)}, bf16[4,512,1023]{2,1,0:T(8,128)(2,1)}, u32[]{:S(2)}) copy-start(bf16[4,512,1023]{2,1,0:T(8,128)(2,1)} %reshape.410) | copy-start | bytes 12570628
  289.6 2.2 copy-start.2
  291.8 1.4 copy-start.10
  304.2 64.6 %all-to-all-start.2 = ((f32[128,2,16,128]{3,2,1,0:T(8,128)}), f32[128,2,16,128]{3,2,1,0:T(8,128)S(1)}, u32[]{:S(2)}, u32[]{:S(2)}) async-start(f32[128,2,16,128]{3,2,1,0:T(8,128)} %copy.50), calls=%async_computation.2 | async-start | bytes 4194304 | tf_op jit(solution)/shard_map/all_to_all | solution.py:124
Sparse Core Ops, SparseCore 0:
  134.2 142.3 all-gather.1
